TPU v7x, 32 devices: a whole 2x2x4 slice. The times are simulated.
32 devices in a mesh: row: 4 (over z), col: 8 (over y, x, core).
Axes of the slice: x: 2, y: 2, z: 4, core: 2. Of those that a mesh axis runs over, the one named last changes fastest.
Arguments:
- load_amp: float32 [2048, 4096], P('row', 'col'), may hold values from 0.05 to 1
- load_mask: int32 [2048, 4096], P('row', 'col'), may hold values 0 or 1
- leak: float32 [2048, 4096], P('row', 'col'), may hold values from 0.001 to 0.05
- coarse_leak: float32 [512, 1024], P('row', 'col'), may hold values from 0.01 to 0.5
- coarse_init: float32 [512, 1024], P('row', 'col'), may hold values from 0 to 1
- via_fine: int32 [4, 8192], P('row', 'col'), may hold values from 0 to 262143
- via_coarse: int32 [4, 8192], P('row', 'col'), may hold values from 0 to 131071, as said below
- via_count: int32 [4, 64], P('row', 'col'), may hold values from 0 to 128, as said below
Outputs:
- fine_drop: float32 [2048, 4096], P('row', 'col')
- coarse_drop: float32 [512, 1024], P('row', 'col')
Inputs may be any that keep to these rules, and one draw needn't show every extreme that they name: `via_coarse`: slot s of a tile names a coarse node whose stored column lies in s // 128 * 128 to s // 128 * 128 + 127. `via_count`: slots of an owner past its count are padding and carry arbitrary indices. In each tile row some owner gets 128 live slots from every tile of that row.
All inputs are finite; a program needn't handle non-finite values. No bound on the sum of `load_mask` on one device may be relied on, other than what follows from the above.
Results may differ from a plain program's by a relative error of at most 0.00022.
Values sent between devices are 32-bit elements; how exact they have to be, the bound alone decides.
A program may use at most 64 MiB of HBM per device.

v0:
```python
import jax
import jax.numpy as jnp
from jax import lax
from jax.sharding import PartitionSpec as P

GROUP = 16
ITERS = 4
CSWEEP = 2


via_conductance = 2.0
coarse_conductance = 4.0
relaxation = 0.8


def extended(block, sides, width, periodic):
    for axis, dim in sides:
        count = lax.axis_size(axis)
        forward = [(i, i + 1) for i in range(count - 1)]
        if periodic:
            forward.append((count - 1, 0))
        backward = [(target, source) for source, target in forward]
        low = lax.ppermute(
            lax.slice_in_dim(block, block.shape[dim] - width, None, axis=dim), axis, forward
        )
        high = lax.ppermute(lax.slice_in_dim(block, 0, width, axis=dim), axis, backward)
        block = jnp.concatenate([low, block, high], axis=dim)
    return block


def fine_apply(field, diagonal):
    padded = extended(field, (("row", 0), ("col", 1)), 1, False)
    beside = padded[2:, 1:-1] + padded[:-2, 1:-1] + padded[1:-1, 2:] + padded[1:-1, :-2]
    return diagonal * field - beside


def coarse_apply(volt, diagonal):
    block_rows, block_cols = volt.shape
    groups = block_cols // GROUP
    stacked = extended(volt, (("row", 0),), 1, False)
    up_down = stacked[2:] + stacked[:-2]
    grouped = volt.reshape(block_rows, groups, GROUP)
    seam = jnp.stack([grouped[:, :, 0], grouped[:, :, GROUP - 1]], axis=0)
    edges = extended(seam, (("col", 0),), 1, True)
    from_left = edges[0]
    from_right = edges[3]
    place = lax.axis_index("col")
    width = lax.axis_size("col")
    zero_col = jnp.zeros((block_rows, 1), jnp.float32)
    left_turned = jnp.concatenate([zero_col, from_left[:, :-1]], axis=1)
    from_left = jnp.where(place == 0, left_turned, from_left)
    right_turned = jnp.concatenate([from_right[:, 1:], zero_col], axis=1)
    from_right = jnp.where(place == width - 1, right_turned, from_right)
    left_full = jnp.concatenate([from_left[:, :, None], grouped[:, :, :-1]], axis=2).reshape(
        block_rows, block_cols
    )
    right_full = jnp.concatenate([grouped[:, :, 1:], from_right[:, :, None]], axis=2).reshape(
        block_rows, block_cols
    )
    return diagonal * volt - coarse_conductance * (up_down + left_full + right_full)


def paired_sum(first, second):
    return lax.psum((jnp.sum(first), jnp.sum(second)), ("row", "col"))


def per_device(
    load_amp, load_mask, leak, coarse_leak, coarse_init, via_fine, via_coarse, via_count
):
    tile_rows, tile_cols = leak.shape
    block_rows, block_cols = coarse_leak.shape
    owners = lax.axis_size("col")
    slot_count = via_fine.shape[1]
    per_owner = slot_count // owners
    row_width = block_cols * owners
    slot_all = jnp.arange(slot_count, dtype=jnp.int32)
    position = slot_all % per_owner
    live = position < jnp.repeat(via_count[0], per_owner)
    weight = jnp.where(live, via_conductance, 0.0).astype(jnp.float32)
    fine_index = via_fine[0]
    coarse_index = via_coarse[0]
    via_diag = jnp.zeros(tile_rows * tile_cols, jnp.float32).at[fine_index].add(weight)
    fine_diag = 4.0 + leak + via_diag.reshape(tile_rows, tile_cols)
    count_local = jnp.zeros(block_rows * row_width, jnp.float32).at[coarse_index].add(weight)
    coarse_count = lax.psum_scatter(
        count_local.reshape(block_rows, row_width), "col", scatter_dimension=1, tiled=True
    )
    coarse_diag = 4.0 * coarse_conductance + coarse_leak + coarse_count
    load = load_amp * load_mask.astype(jnp.float32)
    volt = coarse_init
    solution = jnp.zeros((tile_rows, tile_cols), jnp.float32)
    gathered = lax.all_gather(volt, "col", axis=1, tiled=True)
    at_via = gathered.reshape(-1)[coarse_index]
    injected = jnp.zeros(tile_rows * tile_cols, jnp.float32).at[fine_index].add(weight * at_via)
    rhs = load + injected.reshape(tile_rows, tile_cols)
    residual = rhs - fine_apply(solution, fine_diag)
    precond = residual / fine_diag
    image = fine_apply(precond, fine_diag)
    product, curvature = paired_sum(residual * precond, image * precond)
    alpha = product / curvature
    direction = precond
    along = image
    for iteration in range(ITERS):
        solution = solution + alpha * direction
        residual = residual - alpha * along
        if iteration + 1 < ITERS:
            precond = residual / fine_diag
            image = fine_apply(precond, fine_diag)
            renewed, curvature = paired_sum(residual * precond, image * precond)
            ratio = renewed / product
            alpha = renewed / (curvature - ratio * renewed / alpha)
            direction = precond + ratio * direction
            along = image + ratio * along
            product = renewed
    at_fine = weight * solution.reshape(-1)[fine_index]
    partial_block = jnp.zeros(block_rows * row_width, jnp.float32).at[coarse_index].add(at_fine)
    sources = lax.psum_scatter(
        partial_block.reshape(block_rows, row_width), "col", scatter_dimension=1, tiled=True
    )
    for sweep_turn in range(CSWEEP):
        volt = volt + relaxation * (sources - coarse_apply(volt, coarse_diag)) / coarse_diag
    return (solution, volt)


def solution(mesh):
    in_specs = (
        P("row", "col"),
        P("row", "col"),
        P("row", "col"),
        P("row", "col"),
        P("row", "col"),
        P("row", "col"),
        P("row", "col"),
        P("row", "col"),
    )
    out_specs = (P("row", "col"), P("row", "col"))
    return jax.shard_map(
        per_device, mesh=mesh, in_specs=in_specs, out_specs=out_specs, check_vma=False
    )
```

profile of v0, /device:TPU:0, one launch (start us, length us, event | category | flops | bytes accessed | tf_op | source)
XLA Modules:
  0.0 400.2 jit_solution(1084697743863416688)
XLA Ops:
  8.5 5.6 %collective-permute-start.1 = (f32[1,512]{1,0:T(1,128)S(1)}, f32[1,512]{1,0:T(1,128)S(1)}, u32[]{:S(2)}, u32[]{:S(2)}) collective-permute-start(f32[1,512]{1,0:T(1,128)S(1)} %broadcast.77), channel_id=1, source_target_pairs={{0,8},{8,16},{16,24},{1,9},{9,17},{17,25},{2,10},{10,18},{18,26},{... | collective-permute-start | bytes 6152 | tf_op jit(solution)/shard_map/ppermute | solution.py:23
  14.8 11.7 %all_gather.3 = f32[128,1024]{1,0:T(8,128)S(1)} all-gather(f32[128,128]{1,0:T(8,128)} %param.12), channel_id=1, replica_groups=mesh['row'=4,'col'=8] {'col'}, dimensions={1}, use_global_device_ids=true | all-gather | bytes 589824 | tf_op jit(solution)/shard_map/all_gather | solution.py:92
  26.6 6.2 %gather_fusion = f32[1024]{0:T(1024)S(1)} fusion(f32[131072]{0:T(1024)S(1)} %bitcast.53, s32[1024]{0:T(1024)S(1)} %broadcast_clamp_fusion.1), kind=kCustom, calls=%fused_computation | custom fusion | bytes 12288 | tf_op jit(solution)/shard_map/gather | solution.py:93
  34.4 3.7 collective-permute-start.3
  38.2 6.2 %scatter_custom_fusion.1 = f32[262144]{0:T(1024)S(1)} fusion(s32[1024]{0:T(1024)S(1)} %bitcast.75, f32[1024]{0:T(1024)S(1)} %get-tuple-element.61, f32[]{:T(128)} %constant.12.clone.1), kind=kCustom, calls=%fused_computation.82 | custom fusion | flops 1024 | bytes 1048580 | tf_op jit(solution)/shard_map/scatter-add | solution.py:82
  45.6 6.2 %scatter_custom_fusion = f32[262144]{0:T(1024)S(1)} fusion(s32[1024]{0:T(1024)S(1)} %bitcast.76, f32[1024]{0:T(1024)S(1)} %get-tuple-element.62, f32[]{:T(128)} %constant.12.clone.1), kind=kCustom, calls=%fused_computation.84 | custom fusion | flops 1024 | bytes 1048580 | tf_op jit(solution)/shard_map/scatter-add | solution.py:94
  52.9 3.4 fusion.61
  57.6 4.5 %collective-permute-start.5 = (f32[1,512]{1,0:T(1,128)S(1)}, f32[1,512]{1,0:T(1,128)S(1)}, u32[]{:S(2)}, u32[]{:S(2)}) collective-permute-start(f32[1,512]{1,0:T(1,128)S(1)} %get-tuple-element.47), channel_id=1, source_target_pairs={{0,8},{8,16},{16,24},{1,9},{9,17},{17,25},{2,10},{10,18},{18,26},{... | collective-permute-start | bytes 6152 | tf_op jit(solution)/shard_map/ppermute | solution.py:23
  64.9 3.0 collective-permute-start.7
  70.5 46.7 %all-reduce.9 = (f32[]{:T(128)}, f32[]{:T(128)}) all-reduce(f32[]{:T(128)} %get-tuple-element.11, f32[]{:T(128)} %get-tuple-element.10), channel_id=1, replica_groups=mesh['row'=4,'col'=8] {'row','col'}, use_global_device_ids=true, to_apply=%region_3.4 | all-reduce | flops 2 | bytes 16 | tf_op jit(solution)/shard_map/psum | solution.py:64
  121.5 4.5 %collective-permute-start.9 = (f32[1,512]{1,0:T(1,128)S(1)}, f32[1,512]{1,0:T(1,128)S(1)}, u32[]{:S(2)}, u32[]{:S(2)}) collective-permute-start(f32[1,512]{1,0:T(1,128)S(1)} %get-tuple-element.45), channel_id=1, source_target_pairs={{0,8},{8,16},{16,24},{1,9},{9,17},{17,25},{2,10},{10,18},{18,26},{... | collective-permute-start | bytes 6152 | tf_op jit(solution)/shard_map/ppermute | solution.py:23
  135.4 46.5 %all-reduce.8 = (f32[]{:T(128)}, f32[]{:T(128)}) all-reduce(f32[]{:T(128)} %get-tuple-element.9, f32[]{:T(128)} %get-tuple-element.8), channel_id=1, replica_groups=mesh['row'=4,'col'=8] {'row','col'}, use_global_device_ids=true, to_apply=%region_7.8 | all-reduce | flops 2 | bytes 16 | tf_op jit(solution)/shard_map/psum | solution.py:64
  190.7 4.5 %collective-permute-start.13 = (f32[1,512]{1,0:T(1,128)S(1)}, f32[1,512]{1,0:T(1,128)S(1)}, u32[]{:S(2)}, u32[]{:S(2)}) collective-permute-start(f32[1,512]{1,0:T(1,128)S(1)} %get-tuple-element.43), channel_id=1, source_target_pairs={{0,8},{8,16},{16,24},{1,9},{9,17},{17,25},{2,10},{10,18},{18,26},{... | collective-permute-start | bytes 6152 | tf_op jit(solution)/shard_map/ppermute | solution.py:23
  198.7 3.8 collective-permute-start.15
  204.7 7.0 %scatter_custom_fusion.3 = f32[131072]{0:T(1024)} fusion(s32[1024]{0:T(1024)} %bitcast.73, f32[1024]{0:T(1024)} %copy-done.14, f32[]{:T(128)} %constant.12.clone.1), kind=kCustom, calls=%fused_computation.101 | custom fusion | flops 1024 | bytes 524800 | tf_op jit(solution)/shard_map/scatter-add | solution.py:84
  216.1 41.9 %all-reduce.7 = (f32[]{:T(128)}, f32[]{:T(128)}) all-reduce(f32[]{:T(128)} %get-tuple-element.7, f32[]{:T(128)} %get-tuple-element.6), channel_id=1, replica_groups=mesh['row'=4,'col'=8] {'row','col'}, use_global_device_ids=true, to_apply=%region_11.12 | all-reduce | flops 2 | bytes 16 | tf_op jit(solution)/shard_map/psum | solution.py:64
  265.9 4.5 %collective-permute-start.17 = (f32[1,512]{1,0:T(1,128)S(1)}, f32[1,512]{1,0:T(1,128)S(1)}, u32[]{:S(2)}, u32[]{:S(2)}) collective-permute-start(f32[1,512]{1,0:T(1,128)S(1)} %get-tuple-element.41), channel_id=1, source_target_pairs={{0,8},{8,16},{16,24},{1,9},{9,17},{17,25},{2,10},{10,18},{18,26},{... | collective-permute-start | bytes 6152 | tf_op jit(solution)/shard_map/ppermute | solution.py:23
  273.8 3.0 collective-permute-start.19
  276.9 5.1 %collective-permute-start.21 = (f32[1,128]{1,0:T(1,128)}, f32[1,128]{1,0:T(1,128)}, u32[]{:S(2)}, u32[]{:S(2)}) collective-permute-start(f32[1,128]{1,0:T(1,128)} %get-tuple-element.56), channel_id=1, source_target_pairs={{0,8},{8,16},{16,24},{1,9},{9,17},{17,25},{2,10},{10,18},{18,26},{... | collective-permute-start | bytes 1544 | tf_op jit(solution)/shard_map/ppermute | solution.py:23
  283.4 43.5 %all-reduce.6 = (f32[]{:T(128)}, f32[]{:T(128)}) all-reduce(f32[]{:T(128)} %get-tuple-element.5, f32[]{:T(128)} %get-tuple-element.4), channel_id=1, replica_groups=mesh['row'=4,'col'=8] {'row','col'}, use_global_device_ids=true, to_apply=%region_15.16 | all-reduce | flops 2 | bytes 16 | tf_op jit(solution)/shard_map/psum | solution.py:64
  333.7 6.1 %gather_fusion.1 = f32[1024]{0:T(1024)S(1)} fusion(f32[262144]{0:T(1024)S(1)} %bitcast.54, s32[1024]{0:T(1024)S(1)} %broadcast_clamp_fusion), kind=kCustom, calls=%fused_computation.1 | custom fusion | bytes 12288 | tf_op jit(solution)/shard_map/gather | solution.py:115
  339.9 6.2 %scatter_custom_fusion.2 = f32[131072]{0:T(1024)S(1)} fusion(s32[1024]{0:T(1024)} %bitcast.74, f32[1024]{0:T(1024)S(1)} %fusion.54, f32[]{:T(128)} %constant.12.clone.1), kind=kCustom, calls=%fused_computation.103 | custom fusion | flops 1024 | bytes 524800 | tf_op jit(solution)/shard_map/scatter-add | solution.py:116
  348.8 33.0 %reduce-scatter.3.cloned.1.call-done = f32[128,128]{1,0:T(8,128)} async-done(((f32[128,1024]{1,0:T(8,128)}), f32[128,128]{1,0:T(8,128)}) %reduce-scatter.3.cloned.1.call-update) | async-done | bytes 65552 | tf_op jit(solution)/shard_map/reduce_scatter | solution.py:117
  386.9 4.5 %collective-permute-start.25 = (f32[1,128]{1,0:T(1,128)S(1)}, f32[1,128]{1,0:T(1,128)S(1)}, u32[]{:S(2)}, u32[]{:S(2)}) collective-permute-start(f32[1,128]{1,0:T(1,128)S(1)} %get-tuple-element.50), channel_id=1, source_target_pairs={{0,8},{8,16},{16,24},{1,9},{9,17},{17,25},{2,10},{10,18},{18,26},{... | collective-permute-start | bytes 1544 | tf_op jit(solution)/shard_map/ppermute | solution.py:23
  (140 shorter events, 60.6 us)
Async XLA Ops:
  7.2 341.6 %reduce-scatter.5.cloned.1.call-start = ((), (), s32[]{:S(2)}) async-start(), calls=%async_computation.3 | async-start | bytes 589824 | tf_op jit(solution)/shard_map/reduce_scatter | solution.py:85
  7.2 25.6 %collective-permute-start = (f32[1,512]{1,0:T(1,128)S(1)}, f32[1,512]{1,0:T(1,128)S(1)}, u32[]{:S(2)}, u32[]{:S(2)}) collective-permute-start(f32[1,512]{1,0:T(1,128)S(1)} %broadcast.77), channel_id=1, source_target_pairs={{8,0},{16,8},{24,16},{9,1},{17,9},{25,17},{10,2},{18,10},{26,18},{... | collective-permute-start | bytes 6152 | tf_op jit(solution)/shard_map/ppermute | solution.py:26
  8.5 24.3 %collective-permute-start.1 = (f32[1,512]{1,0:T(1,128)S(1)}, f32[1,512]{1,0:T(1,128)S(1)}, u32[]{:S(2)}, u32[]{:S(2)}) collective-permute-start(f32[1,512]{1,0:T(1,128)S(1)} %broadcast.77), channel_id=1, source_target_pairs={{0,8},{8,16},{16,24},{1,9},{9,17},{17,25},{2,10},{10,18},{18,26},{... | collective-permute-start | bytes 6152 | tf_op jit(solution)/shard_map/ppermute | solution.py:23
  33.1 19.8 %collective-permute-start.2 = (f32[514,1]{1,0:T(8,128)S(1)}, f32[514,1]{1,0:T(8,128)S(1)}, u32[]{:S(2)}, u32[]{:S(2)}) collective-permute-start(f32[514,1]{1,0:T(8,128)S(1)} %get-tuple-element.39), channel_id=1, source_target_pairs={{1,0},{2,1},{3,2},{4,3},{5,4},{6,5},{7,6},{9,8},{10,9},{11,10},{12... | collective-permute-start | bytes 6176 | tf_op jit(solution)/shard_map/ppermute | solution.py:26
  34.4 18.5 %collective-permute-start.3 = (f32[514,1]{1,0:T(8,128)S(1)}, f32[514,1]{1,0:T(8,128)}, u32[]{:S(2)}, u32[]{:S(2)}) collective-permute-start(f32[514,1]{1,0:T(8,128)S(1)} %get-tuple-element.40), channel_id=1, source_target_pairs={{0,1},{1,2},{2,3},{3,4},{4,5},{5,6},{6,7},{8,9},{9,10},{10,11},{11... | collective-permute-start | bytes 6176 | tf_op jit(solution)/shard_map/ppermute | solution.py:23
  56.3 5.9 %collective-permute-start.4 = (f32[1,512]{1,0:T(1,128)S(1)}, f32[1,512]{1,0:T(1,128)S(1)}, u32[]{:S(2)}, u32[]{:S(2)}) collective-permute-start(f32[1,512]{1,0:T(1,128)S(1)} %get-tuple-element.48), channel_id=1, source_target_pairs={{8,0},{16,8},{24,16},{9,1},{17,9},{25,17},{10,2},{18,10},{26,18},{... | collective-permute-start | bytes 6152 | tf_op jit(solution)/shard_map/ppermute | solution.py:26
  57.6 5.8 %collective-permute-start.5 = (f32[1,512]{1,0:T(1,128)S(1)}, f32[1,512]{1,0:T(1,128)S(1)}, u32[]{:S(2)}, u32[]{:S(2)}) collective-permute-start(f32[1,512]{1,0:T(1,128)S(1)} %get-tuple-element.47), channel_id=1, source_target_pairs={{0,8},{8,16},{16,24},{1,9},{9,17},{17,25},{2,10},{10,18},{18,26},{... | collective-permute-start | bytes 6152 | tf_op jit(solution)/shard_map/ppermute | solution.py:23
  120.2 5.9 %collective-permute-start.8 = (f32[1,512]{1,0:T(1,128)S(1)}, f32[1,512]{1,0:T(1,128)S(1)}, u32[]{:S(2)}, u32[]{:S(2)}) collective-permute-start(f32[1,512]{1,0:T(1,128)S(1)} %get-tuple-element.46), channel_id=1, source_target_pairs={{8,0},{16,8},{24,16},{9,1},{17,9},{25,17},{10,2},{18,10},{26,18},{... | collective-permute-start | bytes 6152 | tf_op jit(solution)/shard_map/ppermute | solution.py:26
  121.5 5.8 %collective-permute-start.9 = (f32[1,512]{1,0:T(1,128)S(1)}, f32[1,512]{1,0:T(1,128)S(1)}, u32[]{:S(2)}, u32[]{:S(2)}) collective-permute-start(f32[1,512]{1,0:T(1,128)S(1)} %get-tuple-element.45), channel_id=1, source_target_pairs={{0,8},{8,16},{16,24},{1,9},{9,17},{17,25},{2,10},{10,18},{18,26},{... | collective-permute-start | bytes 6152 | tf_op jit(solution)/shard_map/ppermute | solution.py:23
  189.4 6.0 %collective-permute-start.12 = (f32[1,512]{1,0:T(1,128)S(1)}, f32[1,512]{1,0:T(1,128)S(1)}, u32[]{:S(2)}, u32[]{:S(2)}) collective-permute-start(f32[1,512]{1,0:T(1,128)S(1)} %get-tuple-element.44), channel_id=1, source_target_pairs={{8,0},{16,8},{24,16},{9,1},{17,9},{25,17},{10,2},{18,10},{26,18},{... | collective-permute-start | bytes 6152 | tf_op jit(solution)/shard_map/ppermute | solution.py:26
  190.7 5.8 %collective-permute-start.13 = (f32[1,512]{1,0:T(1,128)S(1)}, f32[1,512]{1,0:T(1,128)S(1)}, u32[]{:S(2)}, u32[]{:S(2)}) collective-permute-start(f32[1,512]{1,0:T(1,128)S(1)} %get-tuple-element.43), channel_id=1, source_target_pairs={{0,8},{8,16},{16,24},{1,9},{9,17},{17,25},{2,10},{10,18},{18,26},{... | collective-permute-start | bytes 6152 | tf_op jit(solution)/shard_map/ppermute | solution.py:23
  197.4 16.3 %collective-permute-start.14 = (f32[514,1]{1,0:T(8,128)}, f32[514,1]{1,0:T(8,128)S(1)}, u32[]{:S(2)}, u32[]{:S(2)}) collective-permute-start(f32[514,1]{1,0:T(8,128)} %get-tuple-element.33), channel_id=1, source_target_pairs={{1,0},{2,1},{3,2},{4,3},{5,4},{6,5},{7,6},{9,8},{10,9},{11,10},{12... | collective-permute-start | bytes 6176 | tf_op jit(solution)/shard_map/ppermute | solution.py:26
  198.7 15.0 %collective-permute-start.15 = (f32[514,1]{1,0:T(8,128)}, f32[514,1]{1,0:T(8,128)}, u32[]{:S(2)}, u32[]{:S(2)}) collective-permute-start(f32[514,1]{1,0:T(8,128)} %get-tuple-element.34), channel_id=1, source_target_pairs={{0,1},{1,2},{2,3},{3,4},{4,5},{5,6},{6,7},{8,9},{9,10},{10,11},{11... | collective-permute-start | bytes 6176 | tf_op jit(solution)/shard_map/ppermute | solution.py:23
  203.1 144.0 %collective-permute-start.23 = (f32[1,128,8]{1,2,0:T(8,128)}, f32[1,128,8]{1,2,0:T(8,128)}, u32[]{:S(2)}, u32[]{:S(2)}) collective-permute-start(f32[1,128,8]{1,2,0:T(8,128)} %bitcast.11), channel_id=1, source_target_pairs={{1,0},{2,1},{3,2},{4,3},{5,4},{6,5},{7,6},{0,7},{9,8},{10,9},{11,1... | collective-permute-start | bytes 12296 | tf_op jit(solution)/shard_map/ppermute | solution.py:26
  204.7 143.8 %collective-permute-start.22 = (f32[1,128,8]{1,2,0:T(8,128)}, f32[1,128,8]{1,2,0:T(8,128)S(1)}, u32[]{:S(2)}, u32[]{:S(2)}) collective-permute-start(f32[1,128,8]{1,2,0:T(8,128)} %bitcast.7), channel_id=1, source_target_pairs={{0,1},{1,2},{2,3},{3,4},{4,5},{5,6},{6,7},{7,0},{8,9},{9,10},{10,1... | collective-permute-start | bytes 12296 | tf_op jit(solution)/shard_map/ppermute | solution.py:23
  213.6 168.1 %reduce-scatter.3.cloned.1.call-start = ((), (), s32[]{:S(2)}) async-start(), calls=%async_computation.2 | async-start | bytes 589824 | tf_op jit(solution)/shard_map/reduce_scatter | solution.py:117
  264.6 7.7 %collective-permute-start.16 = (f32[1,512]{1,0:T(1,128)S(1)}, f32[1,512]{1,0:T(1,128)S(1)}, u32[]{:S(2)}, u32[]{:S(2)}) collective-permute-start(f32[1,512]{1,0:T(1,128)S(1)} %get-tuple-element.42), channel_id=1, source_target_pairs={{8,0},{16,8},{24,16},{9,1},{17,9},{25,17},{10,2},{18,10},{26,18},{... | collective-permute-start | bytes 6152 | tf_op jit(solution)/shard_map/ppermute | solution.py:26
  265.9 6.5 %collective-permute-start.17 = (f32[1,512]{1,0:T(1,128)S(1)}, f32[1,512]{1,0:T(1,128)S(1)}, u32[]{:S(2)}, u32[]{:S(2)}) collective-permute-start(f32[1,512]{1,0:T(1,128)S(1)} %get-tuple-element.41), channel_id=1, source_target_pairs={{0,8},{8,16},{16,24},{1,9},{9,17},{17,25},{2,10},{10,18},{18,26},{... | collective-permute-start | bytes 6152 | tf_op jit(solution)/shard_map/ppermute | solution.py:23
  271.0 77.7 %collective-permute-start.20 = (f32[1,128]{1,0:T(1,128)}, f32[1,128]{1,0:T(1,128)}, u32[]{:S(2)}, u32[]{:S(2)}) collective-permute-start(f32[1,128]{1,0:T(1,128)} %get-tuple-element.55), channel_id=1, source_target_pairs={{8,0},{16,8},{24,16},{9,1},{17,9},{25,17},{10,2},{18,10},{26,18},{... | collective-permute-start | bytes 1544 | tf_op jit(solution)/shard_map/ppermute | solution.py:26
  273.8 8.2 %collective-permute-start.19 = (f32[514,1]{1,0:T(8,128)S(1)}, f32[514,1]{1,0:T(8,128)S(1)}, u32[]{:S(2)}, u32[]{:S(2)}) collective-permute-start(f32[514,1]{1,0:T(8,128)S(1)} %get-tuple-element.32), channel_id=1, source_target_pairs={{0,1},{1,2},{2,3},{3,4},{4,5},{5,6},{6,7},{8,9},{9,10},{10,11},{11... | collective-permute-start | bytes 6176 | tf_op jit(solution)/shard_map/ppermute | solution.py:23
  276.9 71.8 %collective-permute-start.21 = (f32[1,128]{1,0:T(1,128)}, f32[1,128]{1,0:T(1,128)}, u32[]{:S(2)}, u32[]{:S(2)}) collective-permute-start(f32[1,128]{1,0:T(1,128)} %get-tuple-element.56), channel_id=1, source_target_pairs={{0,8},{8,16},{16,24},{1,9},{9,17},{17,25},{2,10},{10,18},{18,26},{... | collective-permute-start | bytes 1544 | tf_op jit(solution)/shard_map/ppermute | solution.py:23
  382.9 8.6 %collective-permute-start.26 = (f32[1,128,8]{1,2,0:T(8,128)S(1)}, f32[1,128,8]{1,2,0:T(8,128)S(1)}, u32[]{:S(2)}, u32[]{:S(2)}) collective-permute-start(f32[1,128,8]{1,2,0:T(8,128)S(1)} %bitcast.78), channel_id=1, source_target_pairs={{0,1},{1,2},{2,3},{3,4},{4,5},{5,6},{6,7},{7,0},{8,9},{9,10},{10,1... | collective-permute-start | bytes 12296 | tf_op jit(solution)/shard_map/ppermute | solution.py:23
  383.0 8.5 %collective-permute-start.27 = (f32[1,128,8]{1,2,0:T(8,128)S(1)}, f32[1,128,8]{1,2,0:T(8,128)S(1)}, u32[]{:S(2)}, u32[]{:S(2)}) collective-permute-start(f32[1,128,8]{1,2,0:T(8,128)S(1)} %bitcast.79), channel_id=1, source_target_pairs={{1,0},{2,1},{3,2},{4,3},{5,4},{6,5},{7,6},{0,7},{9,8},{10,9},{11,1... | collective-permute-start | bytes 12296 | tf_op jit(solution)/shard_map/ppermute | solution.py:26
  385.6 6.1 %collective-permute-start.24 = (f32[1,128]{1,0:T(1,128)S(1)}, f32[1,128]{1,0:T(1,128)S(1)}, u32[]{:S(2)}, u32[]{:S(2)}) collective-permute-start(f32[1,128]{1,0:T(1,128)S(1)} %get-tuple-element.49), channel_id=1, source_target_pairs={{8,0},{16,8},{24,16},{9,1},{17,9},{25,17},{10,2},{18,10},{26,18},{... | collective-permute-start | bytes 1544 | tf_op jit(solution)/shard_map/ppermute | solution.py:26
  (24 other events, 365.7 us)
Sparse Core Ops, SparseCore 0:
  213.8 36.5 reduce-scatter.4
  347.2 34.5 reduce-scatter.2
where the time goes:
time: 402 us; the launch traced here: 400 us
  blocking collectives  190 us (47%)
  starting transfers between devices  69.9 us (17%)
  other arithmetic  50.6 us (13%)
  waiting for transfers between devices  40.1 us (10%)
  between operations  28.2 us (7%)
  local copies, waits for them, and re-layouts  21.2 us (5%)
    psum x4, blocking collectives, paired_sum(): return lax.psum((jnp.sum(first), jnp.sum(second)), ('row', 'col'))  179 us
    ppermute x14, starting transfers between devices, extended(): lax.ppermute(lax.slice_in_dim(block, block.shape[dim] - width, None, axis...  50.1 us
    reduce_scatter x1, waiting for transfers between devices, per_device(): lax.psum_scatter(partial_block.reshape(block_rows, row_width), 'col', sca...  33 us
    ppermute x14, starting transfers between devices, extended(): lax.ppermute(lax.slice_in_dim(block, 0, width, axis=dim), axis, backward)  19.7 us
    all_gather x1, blocking collectives, per_device(): gathered = lax.all_gather(volt, 'col', axis=1, tiled=True)  11.7 us
    div x4, other arithmetic, per_device(): precond = residual / fine_diag  10.8 us
  transfers between devices with their start and end apart: 30, of which 7 were waited for; matrix products, arithmetic and copies ran while one was open for 14% of the time, Pallas kernels for 0%

commit v1 on v0

v1 whole, which is shorter than its diff:
```python
import functools
import jax
import jax.numpy as jnp
from jax import lax
from jax.experimental import pallas as pl
from jax.experimental.pallas import tpu as pltpu
from jax.sharding import PartitionSpec as P

GROUP = 16
ITERS = 4
LANES = 128

via_conductance = 2.0
coarse_conductance = 4.0
relaxation = 0.8

F32 = jnp.float32
BF16 = jnp.bfloat16


def divide(value, by):
    if by & (by - 1) == 0:
        return lax.shift_right_logical(value, by.bit_length() - 1)
    return value // by


def remainder(value, by):
    if by & (by - 1) == 0:
        return value & (by - 1)
    return value % by


def halves(value):
    high = value.astype(BF16).astype(F32)
    return high, value - high


def dot(a, b):
    return jnp.dot(a, b, preferred_element_type=F32)


def chunk_of(rows, top):
    size = top
    while rows % size:
        size -= 8
    return size


def kernel(
    R, C,
    amp, mask, leak, cleak, cinit, vf, vc, cnt,
    x_out, c_out,
    msg_out, msg_in, val_out, val_in, fval_out, fval_in,
    B, Bt, dv, V, Y, rhs,
    E, ET, H, rtop, rbot, rcorner,
    red_out, red_in, red2_out, red2_in,
    volt1, crow_top, crow_bot, cleft, cright,
    send_sem, recv_sem,
):
    row, col = lax.axis_index("row"), lax.axis_index("col")
    TR, TC = leak.shape
    BR, BC = cleak.shape
    S = vf.shape[1]
    per = S // C
    up, down = lax.rem(row + R - 1, R), lax.rem(row + 1, R)
    left, right = lax.rem(col + C - 1, C), lax.rem(col + 1, C)

    barrier = pltpu.get_barrier_semaphore()
    peers = [(row, lax.rem(col + d, C)) for d in range(1, C)]
    peers += [(lax.rem(row + d, R), col) for d in range(1, R)]
    peers += [(u, s) for u in (up, down) for s in (left, right)]
    for peer in peers:
        pl.semaphore_signal(barrier, inc=1, device_id=peer, device_id_type=pl.DeviceIdType.MESH)

    count = [0]
    pending = []

    def send(src, dst, device):
        n = count[0]
        count[0] += 1
        copy = pltpu.make_async_remote_copy(
            src_ref=src, dst_ref=dst, send_sem=send_sem.at[n], recv_sem=recv_sem.at[n],
            device_id=device, device_id_type=pl.DeviceIdType.MESH,
        )
        copy.start()
        pending.append(copy)
        return copy

    lane = lax.broadcasted_iota(jnp.int32, (1, per), 1)
    weight = jnp.concatenate(
        [jnp.where(lane < cnt[0, o], via_conductance, 0.0).astype(F32) for o in range(C)], axis=1
    )
    node = vc[...]
    node_row = divide(node, BC * C).astype(F32)
    node_col = remainder(node, BC).astype(F32)
    for o in range(C):
        cut = slice(o * per, (o + 1) * per)
        msg_out[o, 0:1, :] = node_row[:, cut]
        msg_out[o, 1:2, :] = node_col[:, cut]
        msg_out[o, 2:3, :] = weight[:, cut]
        msg_out[o, 3:8, :] = jnp.zeros((5, per), F32)
    msg_in[col] = msg_out[col]
    for n in range(2):
        H[n] = jnp.zeros((LANES, TR), F32)
    pl.semaphore_wait(barrier, len(peers))

    messages = [
        send(msg_out.at[lax.rem(col + d, C)], msg_in.at[col], (row, lax.rem(col + d, C)))
        for d in range(1, C)
    ]

    def coarse_send(ref, n):
        return [
            send(ref.at[pl.ds(0, 8)], crow_bot.at[n], (up, col)),
            send(ref.at[pl.ds(BR - 8, 8)], crow_top.at[n], (down, col)),
            send(ref, cright.at[n], (row, left)),
            send(ref, cleft.at[n], (row, right)),
        ]

    coarse0 = coarse_send(cinit, 0)

    fine = vf[...]
    fine_row = divide(fine, TC)
    fine_col = remainder(fine, TC)
    step = 64

    def build_cols(i, carry):
        at = pl.ds(pl.multiple_of(i * step, step), step)
        place = lax.broadcasted_iota(jnp.int32, (step, S), 0) + i * step
        B[at, :] = jnp.where(place == fine_col, 1.0, 0.0).astype(BF16)
        return carry

    lax.fori_loop(0, TC // step, build_cols, 0)
    lanes = lax.broadcasted_iota(jnp.int32, (per, TC), 1).astype(F32)
    for o in range(C):
        cut = slice(o * per, (o + 1) * per)
        turned = jnp.broadcast_to(fine_col[:, cut].astype(F32), (LANES, per)).T
        wide = jnp.concatenate([turned] * (TC // LANES), axis=1)
        Bt[cut, :] = jnp.where(wide == lanes, 1.0, 0.0).astype(BF16)

    zero_pad = jnp.zeros((8, TC + LANES), F32)
    for n in range(ITERS):
        V[n, 0:8, :] = zero_pad
        V[n, TR + 24 : TR + 32, :] = zero_pad

    def diagonal(i, carry):
        at = pl.ds(pl.multiple_of(i * step, step), step)
        inner = pl.ds(pl.multiple_of(16 + i * step, 8), step)
        place = lax.broadcasted_iota(jnp.int32, (step, S), 0) + i * step
        match = place == fine_row
        value = 4.0 + leak[at, :] + dot(jnp.where(match, weight, 0.0).astype(BF16), Bt[...])
        dv[inner, 0:TC] = 1.0 / value
        return carry

    lax.fori_loop(0, TR // step, diagonal, 0)

    low_side = lax.broadcasted_iota(jnp.int32, (TR, LANES), 1) < LANES // 2

    def halo_send(F, n):
        edge = jnp.where(low_side, F[16 : 16 + TR, 0:LANES], F[16 : 16 + TR, TC - LANES : TC])
        E[n] = edge
        ET[n] = edge.T
        return [
            send(F.at[pl.ds(16, 8), pl.ds(0, TC)], rbot.at[n], (up, col)),
            send(F.at[pl.ds(TR + 8, 8), pl.ds(0, TC)], rtop.at[n], (down, col)),
            send(ET.at[n, pl.ds(0, 8)], H.at[n, pl.ds(0, 8)], (row, left)),
            send(ET.at[n, pl.ds(LANES - 8, 8)], H.at[n, pl.ds(LANES - 8, 8)], (row, right)),
            send(E.at[n, pl.ds(0, 8)], rcorner.at[n, 3], (up, left)),
            send(E.at[n, pl.ds(0, 8)], rcorner.at[n, 2], (up, right)),
            send(E.at[n, pl.ds(TR - 8, 8)], rcorner.at[n, 1], (down, left)),
            send(E.at[n, pl.ds(TR - 8, 8)], rcorner.at[n, 0], (down, right)),
        ]

    top_ok, bot_ok = row > 0, row < R - 1
    left_ok, right_ok = col > 0, col < C - 1

    def keep(ok, value):
        return value * jnp.where(ok, 1.0, 0.0).astype(F32)

    def halo_land(F, n, copies):
        for copy in copies:
            copy.wait_recv()
        F[8:16, 0:TC] = keep(top_ok, rtop[n])
        F[TR + 16 : TR + 24, 0:TC] = keep(bot_ok, rbot[n])
        side = H[n].T
        F[16 : 16 + TR, TC : TC + LANES] = jnp.where(
            low_side, keep(right_ok, side), keep(left_ok, side)
        )
        low8 = lax.broadcasted_iota(jnp.int32, (8, LANES), 1)
        near_low, near_high = low8 < 8, low8 >= LANES - 8

        def corner(ok, lo, hi):
            return keep(
                ok,
                jnp.where(near_low, keep(right_ok, lo), 0.0)
                + jnp.where(near_high, keep(left_ok, hi), 0.0),
            )

        F[8:16, TC : TC + LANES] = corner(top_ok, rcorner[n, 1], rcorner[n, 0])
        F[TR + 16 : TR + 24, TC : TC + LANES] = corner(bot_ok, rcorner[n, 3], rcorner[n, 2])

    for copy in messages:
        copy.wait_recv()
    heard = [msg_in[t] for t in range(C)]
    in_row = jnp.concatenate([m[0:1] for m in heard], axis=1).astype(jnp.int32)
    in_col = jnp.concatenate([m[1:2] for m in heard], axis=1).astype(jnp.int32)
    in_weight = jnp.concatenate([m[2:3] for m in heard], axis=1)
    place_r = lax.broadcasted_iota(jnp.int32, (BR, S), 0)
    place_c = lax.broadcasted_iota(jnp.int32, (BC, S), 0)
    row_hit = place_r == in_row
    col_hot = jnp.where(place_c == in_col, 1.0, 0.0).astype(BF16)
    hi, lo = halves(cinit[...])
    seen = dot(hi.astype(BF16), col_hot) + dot(lo.astype(BF16), col_hot)
    at_via = jnp.sum(jnp.where(row_hit, seen, 0.0), axis=0, keepdims=True)
    for t in range(C):
        val_out[t] = at_via[:, t * per : (t + 1) * per]
    val_in[col] = val_out[col]
    values = [
        send(val_out.at[lax.rem(col + d, C)], val_in.at[col], (row, lax.rem(col + d, C)))
        for d in range(1, C)
    ]

    dinv_copies = halo_send(dv, 0)

    def onto_coarse(amount):
        spread = jnp.where(row_hit, amount, 0.0).astype(BF16)
        return lax.dot_general(spread, col_hot, (((1,), (1,)), ((), ())), preferred_element_type=F32)

    coarse_diag = 4.0 * coarse_conductance + cleak[...] + onto_coarse(in_weight)

    for copy in values:
        copy.wait_recv()
    drops = weight * jnp.concatenate([val_in[o] for o in range(C)], axis=1)
    drop_hi, drop_lo = halves(drops)

    def inject(i, carry):
        at = pl.ds(pl.multiple_of(i * step, step), step)
        inner = pl.ds(pl.multiple_of(16 + i * step, 8), step)
        place = lax.broadcasted_iota(jnp.int32, (step, S), 0) + i * step
        match = place == fine_row
        added = dot(jnp.where(match, drop_hi, 0.0).astype(BF16), Bt[...])
        added += dot(jnp.where(match, drop_lo, 0.0).astype(BF16), Bt[...])
        value = amp[at, :] * mask[at, :].astype(F32) + added
        rhs[at, :] = value
        V[0, inner, 0:TC] = value * dv[inner, 0:TC]
        return carry

    lax.fori_loop(0, TR // step, inject, 0)
    first_copies = halo_send(V.at[0], 1)
    halo_land(dv, 0, dinv_copies)
    halo_land(V.at[0], 1, first_copies)

    rows = chunk_of(TR + 16, 48)
    width = TC + LANES

    def around(k, start, size):
        tall = V[k, pl.ds(pl.multiple_of(start - 8, 8), size + 16), :]
        mid = tall[8 : 8 + size]
        total = pltpu.roll(tall, 1, 0)[8 : 8 + size] + pltpu.roll(tall, size + 15, 0)[8 : 8 + size]
        return total + pltpu.roll(mid, 1, 1) + pltpu.roll(mid, width - 1, 1)

    for k in range(ITERS - 1):

        def advance(i, carry, k=k):
            start = pl.multiple_of(8 + i * rows, 8)
            near = around(k, start, rows)
            Y[k, pl.ds(start, rows), :] = near
            fresh = dv[pl.ds(start, rows), :] * near
            if k:
                fresh = 2.0 * fresh - V[k - 1, pl.ds(start, rows), :]
            V[k + 1, pl.ds(start, rows), :] = fresh
            return carry

        lax.fori_loop(0, (TR + 16) // rows, advance, 0)

    pairs = [(j, k) for k in range(ITERS) for j in range(k + 1)]
    sums = len(pairs) + ITERS

    def fold(value):
        total = value[:, 0:LANES]
        for n in range(1, TC // LANES):
            total = total + value[:, n * LANES : (n + 1) * LANES]
        return total

    def gram(i, carry):
        at = pl.ds(pl.multiple_of(i * 8, 8), 8)
        start = pl.multiple_of(16 + i * 8, 8)
        inner = pl.ds(start, 8)
        v = [V[k, inner, 0:TC] for k in range(ITERS)]
        y = [Y[k, inner, 0:TC] for k in range(ITERS - 1)]
        y.append(around(ITERS - 1, start, 8)[:, 0:TC])
        w = [rhs[at, :], y[0]]
        for k in range(2, ITERS):
            w.append(2.0 * y[k - 1] - w[k - 2])
        applied = [w[k] - y[k] for k in range(ITERS)]
        fresh = [fold(v[j] * applied[k]) for j, k in pairs] + [fold(w[0] * v[k]) for k in range(ITERS)]
        return tuple(a + b for a, b in zip(carry, fresh))

    totals = lax.fori_loop(0, TR // 8, gram, tuple(jnp.zeros((8, LANES), F32) for _ in range(sums)))
    red_out[...] = jnp.zeros(red_out.shape, F32)
    for n, total in enumerate(totals):
        red_out[n : n + 1, :] = jnp.sum(total, axis=0, keepdims=True)
    copies = [
        send(red_out, red_in.at[d - 1], (row, lax.rem(col + d, C))) for d in range(1, C)
    ]
    total = red_out[...]
    for d, copy in enumerate(copies):
        copy.wait_recv()
        total = total + red_in[d]
    red2_out[...] = total
    copies = [
        send(red2_out, red2_in.at[d - 1], (lax.rem(row + d, R), col)) for d in range(1, R)
    ]
    for d, copy in enumerate(copies):
        copy.wait_recv()
        total = total + red2_in[d]
    total = jnp.sum(total, axis=1, keepdims=True)
    number = [total[n : n + 1, :] for n in range(sums)]

    matrix = [[None] * (ITERS + 1) for _ in range(ITERS)]
    for n, (j, k) in enumerate(pairs):
        matrix[j][k] = matrix[k][j] = number[n]
    for k in range(ITERS):
        matrix[k][ITERS] = number[len(pairs) + k]
    for i in range(ITERS):
        inverse = 1.0 / matrix[i][i]
        for k in range(i + 1, ITERS + 1):
            matrix[i][k] = matrix[i][k] * inverse
        for j in range(i + 1, ITERS):
            for k in range(i + 1, ITERS + 1):
                matrix[j][k] = matrix[j][k] - matrix[j][i] * matrix[i][k]
    coef = [None] * ITERS
    for i in reversed(range(ITERS)):
        coef[i] = matrix[i][ITERS]
        for k in range(i + 1, ITERS):
            coef[i] = coef[i] - matrix[i][k] * coef[k]

    def finish(i, carry):
        at = pl.ds(pl.multiple_of(i * step, step), step)
        inner = pl.ds(pl.multiple_of(16 + i * step, 8), step)
        value = coef[0] * V[0, inner, 0:TC]
        for k in range(1, ITERS):
            value = value + coef[k] * V[k, inner, 0:TC]
        x_out[at, :] = value
        high, low = halves(value)
        seen = dot(high.astype(BF16), B[...]) + dot(low.astype(BF16), B[...])
        place = lax.broadcasted_iota(jnp.int32, (step, S), 0) + i * step
        return carry + jnp.sum(jnp.where(place == fine_row, seen, 0.0), axis=0, keepdims=True)

    at_fine = lax.fori_loop(0, TR // step, finish, jnp.zeros((1, S), F32))
    for o in range(C):
        fval_out[o] = at_fine[:, o * per : (o + 1) * per]
    fval_in[col] = fval_out[col]
    copies = [
        send(fval_out.at[lax.rem(col + d, C)], fval_in.at[col], (row, lax.rem(col + d, C)))
        for d in range(1, C)
    ]

    place = lax.broadcasted_iota(jnp.int32, (BR, BC), 1)
    place_v = lax.broadcasted_iota(jnp.int32, (BR, BC), 0)
    within = remainder(place, GROUP)

    def beside(volt, n):
        above = jnp.where(place_v == 0, keep(top_ok, crow_top[n, 7:8, :]), pltpu.roll(volt, 1, 0))
        below = jnp.where(
            place_v == BR - 1, keep(bot_ok, crow_bot[n, 0:1, :]), pltpu.roll(volt, BR - 1, 0)
        )
        far_left, far_right = cleft[n], cright[n]
        turned_left = jnp.where(place == 0, 0.0, pltpu.roll(far_left, 1, 1))
        plain_left = pltpu.roll(far_left, BC - GROUP + 1, 1)
        from_left = jnp.where(left_ok, plain_left, turned_left)
        turned_right = jnp.where(place == BC - 1, 0.0, pltpu.roll(far_right, BC - 1, 1))
        plain_right = pltpu.roll(far_right, GROUP - 1, 1)
        from_right = jnp.where(right_ok, plain_right, turned_right)
        before = jnp.where(within == 0, from_left, pltpu.roll(volt, 1, 1))
        after = jnp.where(within == GROUP - 1, from_right, pltpu.roll(volt, BC - 1, 1))
        return above + below + before + after

    for copy in coarse0:
        copy.wait_recv()
    volt = cinit[...]
    scale = relaxation / coarse_diag
    partial = volt + scale * (coarse_conductance * beside(volt, 0) - coarse_diag * volt)
    for copy in copies:
        copy.wait_recv()
    amount = in_weight * jnp.concatenate([fval_in[t] for t in range(C)], axis=1)
    hi, lo = halves(amount)
    sources = onto_coarse(hi) + onto_coarse(lo)
    volt = partial + scale * sources
    volt1[...] = volt
    coarse1 = coarse_send(volt1, 1)
    partial = volt + scale * (sources - coarse_diag * volt)
    for copy in coarse1:
        copy.wait_recv()
    c_out[...] = partial + scale * (coarse_conductance * beside(volt, 1))
    for copy in pending:
        copy.wait_send()


def per_device(R, C, load_amp, load_mask, leak, coarse_leak, coarse_init, via_fine, via_coarse, via_count):
    TR, TC = leak.shape
    BR, BC = coarse_leak.shape
    S = via_fine.shape[1]
    per = S // C
    copies = 4 * (C - 1) + (R - 1) + 24
    vmem = pl.BlockSpec(memory_space=pltpu.VMEM)
    ext = (TR + 32, TC + LANES)
    return pl.pallas_call(
        functools.partial(kernel, R, C),
        out_shape=(jax.ShapeDtypeStruct((TR, TC), F32), jax.ShapeDtypeStruct((BR, BC), F32)),
        in_specs=[vmem] * 7 + [pl.BlockSpec(memory_space=pltpu.SMEM)],
        out_specs=(vmem, vmem),
        scratch_shapes=[
            pltpu.VMEM((C, 8, per), F32), pltpu.VMEM((C, 8, per), F32),
            pltpu.VMEM((C, 1, per), F32), pltpu.VMEM((C, 1, per), F32),
            pltpu.VMEM((C, 1, per), F32), pltpu.VMEM((C, 1, per), F32),
            pltpu.VMEM((TC, S), BF16),
            pltpu.VMEM((S, TC), BF16),
            pltpu.VMEM(ext, F32),
            pltpu.VMEM((ITERS,) + ext, F32),
            pltpu.VMEM((ITERS - 1,) + ext, F32),
            pltpu.VMEM((TR, TC), F32),
            pltpu.VMEM((2, TR, LANES), F32),
            pltpu.VMEM((2, LANES, TR), F32),
            pltpu.VMEM((2, LANES, TR), F32),
            pltpu.VMEM((2, 8, TC), F32),
            pltpu.VMEM((2, 8, TC), F32),
            pltpu.VMEM((2, 4, 8, LANES), F32),
            pltpu.VMEM((16, LANES), F32), pltpu.VMEM((C - 1, 16, LANES), F32),
            pltpu.VMEM((16, LANES), F32), pltpu.VMEM((R - 1, 16, LANES), F32),
            pltpu.VMEM((BR, BC), F32),
            pltpu.VMEM((2, 8, BC), F32), pltpu.VMEM((2, 8, BC), F32),
            pltpu.VMEM((2, BR, BC), F32), pltpu.VMEM((2, BR, BC), F32),
            pltpu.SemaphoreType.DMA((copies,)),
            pltpu.SemaphoreType.DMA((copies,)),
        ],
        compiler_params=pltpu.CompilerParams(
            collective_id=0, has_side_effects=True, vmem_limit_bytes=48 * 1024 * 1024
        ),
    )(load_amp, load_mask, leak, coarse_leak, coarse_init, via_fine, via_coarse, via_count)


def solution(mesh):
    spec = P("row", "col")
    return jax.shard_map(
        functools.partial(per_device, mesh.shape["row"], mesh.shape["col"]),
        mesh=mesh, in_specs=(spec,) * 8, out_specs=(spec, spec), check_vma=False,
    )
```

time: 402 us -> 60.4 us (0.15)
  blocking collectives: 190 us -> 0 us
  starting transfers between devices: 69.9 us -> 0 us
  other arithmetic: 50.6 us -> 0 us
  Pallas kernels: 0 us -> 50.4 us
  waiting for transfers between devices: 40.1 us -> 0 us
  between operations: 28.2 us -> 0.66 us
  local copies, waits for them, and re-layouts: 21.2 us -> 8.97 us
    psum x4 -> x0, blocking collectives: 179 us -> none  [paired_sum(): return lax.psum((jnp.sum(first), jnp.sum(second)), ('row', 'col'))]
    ppermute x28 -> x0, starting transfers between devices: 69.9 us -> none  [the longest x14 50.1 us: extended(): lax.ppermute(lax.slice_in_dim(block, block.shape[dim] - width, None, axis...]
    pallas_call x0 -> x1, Pallas kernels: none -> 50.4 us  [per_device(): pl.pallas_call(functools.partial(kernel, R, C), out_shape=(jax.ShapeDtype...]
    reduce_scatter x2 -> x0, waiting for transfers between devices: 33 us -> none  [the longest x1 33 us: per_device(): lax.psum_scatter(partial_block.reshape(block_rows, row_width), 'col', sca...]
    scatter-add x4 -> x0, other arithmetic: 25.5 us -> none  [the longest x1 6.98 us: per_device(): jnp.zeros(block_rows * row_width, jnp.float32).at[coarse_index].add(weight)]
    gather x2 -> x0, local copies, waits for them, and re-layouts: 12.3 us -> none  [the longest x1 6.15 us: per_device(): at_via = gathered.reshape(-1)[coarse_index]]
    all_gather x1 -> x0, blocking collectives: 11.7 us -> none  [per_device(): gathered = lax.all_gather(volt, 'col', axis=1, tiled=True)]
    div x4 -> x0, other arithmetic: 10.8 us -> none  [per_device(): precond = residual / fine_diag]
  transfers between devices with their start and end apart: 30 -> 0, of which waited for: 7 -> 0; matrix products, arithmetic and copies ran while one was open for 14% -> 0% of each run, Pallas kernels for 0% -> 0%
where the time goes in v1:
time: 60.4 us; the launch traced here: 60 us
  Pallas kernels  50.4 us (83%)
  local copies, waits for them, and re-layouts  8.97 us (15%)
  between operations  0.66 us (1%)
    pallas_call x1, Pallas kernels, per_device(): pl.pallas_call(functools.partial(kernel, R, C), out_shape=(jax.ShapeDtype...  50.4 us
    unnamed x18, local copies, waits for them, and re-layouts  8.97 us

profile of v1, /device:TPU:0, one launch (start us, length us, event | category | flops | bytes accessed | tf_op | source)
XLA Modules:
  0.0 60.0 jit_solution(1287299817311018218)
XLA Ops:
  0.6 0.0 copy-start
  0.6 1.2 %copy-done = f32[512,512]{1,0:T(8,128)S(1)} copy-done((f32[512,512]{1,0:T(8,128)S(1)}, f32[512,512]{1,0:T(8,128)}, u32[]{:S(2)}) %copy-start) | copy-done | bytes 1048600
  1.9 0.0 copy-start.1
  1.9 1.2 %copy-done.1 = s32[512,512]{1,0:T(8,128)S(1)} copy-done((s32[512,512]{1,0:T(8,128)S(1)}, s32[512,512]{1,0:T(8,128)}, u32[]{:S(2)}) %copy-start.1) | copy-done | bytes 1048600
  3.1 0.0 copy-start.2
  3.1 1.2 %copy-done.2 = f32[512,512]{1,0:T(8,128)S(1)} copy-done((f32[512,512]{1,0:T(8,128)S(1)}, f32[512,512]{1,0:T(8,128)}, u32[]{:S(2)}) %copy-start.2) | copy-done | bytes 1048600
  4.3 0.0 copy-start.3
  4.3 0.8 %copy-done.3 = f32[128,128]{1,0:T(8,128)S(1)} copy-done((f32[128,128]{1,0:T(8,128)S(1)}, f32[128,128]{1,0:T(8,128)}, u32[]{:S(2)}) %copy-start.3) | copy-done | bytes 65560
  5.1 0.0 copy-start.4
  5.2 0.8 %copy-done.4 = f32[128,128]{1,0:T(8,128)S(1)} copy-done((f32[128,128]{1,0:T(8,128)S(1)}, f32[128,128]{1,0:T(8,128)}, u32[]{:S(2)}) %copy-start.4) | copy-done | bytes 65560
  6.0 0.0 copy-start.5
  6.0 0.7 %copy-done.5 = s32[1,1024]{1,0:T(1,128)S(1)} copy-done((s32[1,1024]{1,0:T(1,128)S(1)}, s32[1,1024]{1,0:T(1,128)}, u32[]{:S(2)}) %copy-start.5) | copy-done | bytes 4120
  6.7 0.0 copy-start.6
  6.7 0.7 %copy-done.6 = s32[1,1024]{1,0:T(1,128)S(1)} copy-done((s32[1,1024]{1,0:T(1,128)S(1)}, s32[1,1024]{1,0:T(1,128)}, u32[]{:S(2)}) %copy-start.6) | copy-done | bytes 4120
  7.4 0.0 copy-start.7
  7.4 0.7 %copy-done.7 = s32[1,8]{1,0:T(1,128)S(1)} copy-done((s32[1,8]{1,0:T(1,128)S(1)}, s32[1,8]{1,0:T(1,128)}, u32[]{:S(2)}) %copy-start.7) | copy-done | bytes 56
  8.0 50.4 %shard_map.95 = (f32[512,512]{1,0:T(8,128)S(1)}, f32[128,128]{1,0:T(8,128)S(1)}) custom-call(f32[512,512]{1,0:T(8,128)S(1)} %copy-done, s32[512,512]{1,0:T(8,128)S(1)} %copy-done.1, f32[512,512]{1,0:T(8,128)S(1)} %copy-done.2, f32[128,128]{1,0:T(8,128)S(1)} %copy-done.3, f32[128,128]{1,0:T(8,128)S(1)} %copy-done.4, s32[1,1024]{1,0:T(1,128)S(1)} %copy-done.5, ...), custom_call_target="tpu_custom_call" | custom-call | tf_op jit(solution)/shard_map/pallas_call | solution.py:408
  58.4 1.0 %copy.12 = f32[512,512]{1,0:T(8,128)} copy(f32[512,512]{1,0:T(8,128)S(1)} %get-tuple-element.4) | data formatting | bytes 2097152
  59.4 0.6 %copy.13 = f32[128,128]{1,0:T(8,128)} copy(f32[128,128]{1,0:T(8,128)S(1)} %get-tuple-element.5) | data formatting | bytes 131072
Async XLA Ops:
  0.6 1.2 %copy-start = (f32[512,512]{1,0:T(8,128)S(1)}, f32[512,512]{1,0:T(8,128)}, u32[]{:S(2)}) copy-start(f32[512,512]{1,0:T(8,128)} %amp.1) | copy-start | bytes 3145732
  1.9 1.2 %copy-start.1 = (s32[512,512]{1,0:T(8,128)S(1)}, s32[512,512]{1,0:T(8,128)}, u32[]{:S(2)}) copy-start(s32[512,512]{1,0:T(8,128)} %mask.1) | copy-start | bytes 3145732
  3.1 1.2 %copy-start.2 = (f32[512,512]{1,0:T(8,128)S(1)}, f32[512,512]{1,0:T(8,128)}, u32[]{:S(2)}) copy-start(f32[512,512]{1,0:T(8,128)} %leak.1) | copy-start | bytes 3145732
  4.3 0.8 %copy-start.3 = (f32[128,128]{1,0:T(8,128)S(1)}, f32[128,128]{1,0:T(8,128)}, u32[]{:S(2)}) copy-start(f32[128,128]{1,0:T(8,128)} %cleak.1) | copy-start | bytes 196612
  5.1 0.8 %copy-start.4 = (f32[128,128]{1,0:T(8,128)S(1)}, f32[128,128]{1,0:T(8,128)}, u32[]{:S(2)}) copy-start(f32[128,128]{1,0:T(8,128)} %cinit.1) | copy-start | bytes 196612
  6.0 0.7 %copy-start.5 = (s32[1,1024]{1,0:T(1,128)S(1)}, s32[1,1024]{1,0:T(1,128)}, u32[]{:S(2)}) copy-start(s32[1,1024]{1,0:T(1,128)} %vf.1) | copy-start | bytes 12292
  6.7 0.7 %copy-start.6 = (s32[1,1024]{1,0:T(1,128)S(1)}, s32[1,1024]{1,0:T(1,128)}, u32[]{:S(2)}) copy-start(s32[1,1024]{1,0:T(1,128)} %vc.1) | copy-start | bytes 12292
  7.4 0.7 %copy-start.7 = (s32[1,8]{1,0:T(1,128)S(1)}, s32[1,8]{1,0:T(1,128)}, u32[]{:S(2)}) copy-start(s32[1,8]{1,0:T(1,128)} %cnt.1) | copy-start | bytes 100

commit v2 on v1

--- a/solution.py
+++ b/solution.py
@@ -48,16 +48,25 @@
 
 def kernel(
     R, C,
-    amp, mask, leak, cleak, cinit, vf, vc, cnt,
+    amp_in, mask_in, leak_in, cleak_in, cinit_in, vf_in, vc_in, cnt_in,
     x_out, c_out,
+    amp, mask, leak, cleak, cinit, vf, vc, cnt, load_sem, xv,
     msg_out, msg_in, val_out, val_in, fval_out, fval_in,
     B, Bt, dv, V, Y, rhs,
     E, ET, H, rtop, rbot, rcorner,
     red_out, red_in, red2_out, red2_in,
-    volt1, crow_top, crow_bot, cleft, cright,
+    volt1, turn, seam_out, crow_top, crow_bot, cleft, cright,
     send_sem, recv_sem,
 ):
     row, col = lax.axis_index("row"), lax.axis_index("col")
+    sources_of = (cnt_in, vc_in, vf_in, cinit_in, leak_in, cleak_in, amp_in, mask_in)
+    targets_of = (cnt, vc, vf, cinit, leak, cleak, amp, mask)
+    loads = [
+        pltpu.make_async_copy(source, target, load_sem.at[n])
+        for n, (source, target) in enumerate(zip(sources_of, targets_of))
+    ]
+    for load in loads:
+        load.start()
     TR, TC = leak.shape
     BR, BC = cleak.shape
     S = vf.shape[1]
@@ -86,6 +95,8 @@
         pending.append(copy)
         return copy
 
+    loads[0].wait()
+    loads[1].wait()
     lane = lax.broadcasted_iota(jnp.int32, (1, per), 1)
     weight = jnp.concatenate(
         [jnp.where(lane < cnt[0, o], via_conductance, 0.0).astype(F32) for o in range(C)], axis=1
@@ -102,23 +113,7 @@
     msg_in[col] = msg_out[col]
     for n in range(2):
         H[n] = jnp.zeros((LANES, TR), F32)
-    pl.semaphore_wait(barrier, len(peers))
-
-    messages = [
-        send(msg_out.at[lax.rem(col + d, C)], msg_in.at[col], (row, lax.rem(col + d, C)))
-        for d in range(1, C)
-    ]
-
-    def coarse_send(ref, n):
-        return [
-            send(ref.at[pl.ds(0, 8)], crow_bot.at[n], (up, col)),
-            send(ref.at[pl.ds(BR - 8, 8)], crow_top.at[n], (down, col)),
-            send(ref, cright.at[n], (row, left)),
-            send(ref, cleft.at[n], (row, right)),
-        ]
-
-    coarse0 = coarse_send(cinit, 0)
-
+    loads[2].wait()
     fine = vf[...]
     fine_row = divide(fine, TC)
     fine_col = remainder(fine, TC)
@@ -138,21 +133,51 @@
         wide = jnp.concatenate([turned] * (TC // LANES), axis=1)
         Bt[cut, :] = jnp.where(wide == lanes, 1.0, 0.0).astype(BF16)
 
+    pl.semaphore_wait(barrier, len(peers))
+
+    messages = [
+        send(msg_out.at[lax.rem(col + d, C)], msg_in.at[col], (row, lax.rem(col + d, C)))
+        for d in range(1, C)
+    ]
+
+    def coarse_send(ref, n):
+        return [
+            send(ref.at[pl.ds(0, 8)], crow_bot.at[n], (up, col)),
+            send(ref.at[pl.ds(BR - 8, 8)], crow_top.at[n], (down, col)),
+            send(seam_out.at[n, 0], cright.at[n], (row, left)),
+            send(seam_out.at[n, 1], cleft.at[n], (row, right)),
+        ]
+
+    groups = BC // GROUP
+
+    def seams(volt, n):
+        turn[n] = volt.T
+        seam_out[n, 0] = turn[n, pl.ds(0, groups, stride=GROUP), :]
+        seam_out[n, 1] = turn[n, pl.ds(GROUP - 1, groups, stride=GROUP), :]
+
+    loads[3].wait()
+    seams(cinit[...], 0)
+    coarse0 = coarse_send(cinit, 0)
+
     zero_pad = jnp.zeros((8, TC + LANES), F32)
     for n in range(ITERS):
         V[n, 0:8, :] = zero_pad
         V[n, TR + 24 : TR + 32, :] = zero_pad
 
+    loads[4].wait()
+    wide_step = 256 if TR % 256 == 0 else step
+    half_step = wide_step // 2
+
     def diagonal(i, carry):
-        at = pl.ds(pl.multiple_of(i * step, step), step)
-        inner = pl.ds(pl.multiple_of(16 + i * step, 8), step)
-        place = lax.broadcasted_iota(jnp.int32, (step, S), 0) + i * step
+        at = pl.ds(pl.multiple_of(i * wide_step, wide_step), wide_step)
+        inner = pl.ds(pl.multiple_of(16 + i * wide_step, 8), wide_step)
+        place = lax.broadcasted_iota(jnp.int32, (wide_step, S), 0) + i * wide_step
         match = place == fine_row
         value = 4.0 + leak[at, :] + dot(jnp.where(match, weight, 0.0).astype(BF16), Bt[...])
         dv[inner, 0:TC] = 1.0 / value
         return carry
 
-    lax.fori_loop(0, TR // step, diagonal, 0)
+    lax.fori_loop(0, TR // wide_step, diagonal, 0)
 
     low_side = lax.broadcasted_iota(jnp.int32, (TR, LANES), 1) < LANES // 2
 
@@ -226,26 +251,30 @@
         spread = jnp.where(row_hit, amount, 0.0).astype(BF16)
         return lax.dot_general(spread, col_hot, (((1,), (1,)), ((), ())), preferred_element_type=F32)
 
+    loads[5].wait()
     coarse_diag = 4.0 * coarse_conductance + cleak[...] + onto_coarse(in_weight)
 
     for copy in values:
         copy.wait_recv()
+    loads[6].wait()
+    loads[7].wait()
     drops = weight * jnp.concatenate([val_in[o] for o in range(C)], axis=1)
     drop_hi, drop_lo = halves(drops)
 
     def inject(i, carry):
-        at = pl.ds(pl.multiple_of(i * step, step), step)
-        inner = pl.ds(pl.multiple_of(16 + i * step, 8), step)
-        place = lax.broadcasted_iota(jnp.int32, (step, S), 0) + i * step
+        at = pl.ds(pl.multiple_of(i * half_step, half_step), half_step)
+        inner = pl.ds(pl.multiple_of(16 + i * half_step, 8), half_step)
+        place = lax.broadcasted_iota(jnp.int32, (half_step, S), 0) + i * half_step
         match = place == fine_row
-        added = dot(jnp.where(match, drop_hi, 0.0).astype(BF16), Bt[...])
-        added += dot(jnp.where(match, drop_lo, 0.0).astype(BF16), Bt[...])
+        both = [jnp.where(match, part, 0.0).astype(BF16) for part in (drop_hi, drop_lo)]
+        both = dot(jnp.concatenate(both, axis=0), Bt[...])
+        added = both[:half_step] + both[half_step:]
         value = amp[at, :] * mask[at, :].astype(F32) + added
         rhs[at, :] = value
         V[0, inner, 0:TC] = value * dv[inner, 0:TC]
         return carry
 
-    lax.fori_loop(0, TR // step, inject, 0)
+    lax.fori_loop(0, TR // half_step, inject, 0)
     first_copies = halo_send(V.at[0], 1)
     halo_land(dv, 0, dinv_copies)
     halo_land(V.at[0], 1, first_copies)
@@ -254,9 +283,9 @@
     width = TC + LANES
 
     def around(k, start, size):
-        tall = V[k, pl.ds(pl.multiple_of(start - 8, 8), size + 16), :]
-        mid = tall[8 : 8 + size]
-        total = pltpu.roll(tall, 1, 0)[8 : 8 + size] + pltpu.roll(tall, size + 15, 0)[8 : 8 + size]
+        tall = V.at[k, pl.ds(pl.multiple_of(start - 8, 8), size + 16), :]
+        mid = tall[8 : 8 + size, :]
+        total = tall[7 : 7 + size, :] + tall[9 : 9 + size, :]
         return total + pltpu.roll(mid, 1, 1) + pltpu.roll(mid, width - 1, 1)
 
     for k in range(ITERS - 1):
@@ -273,8 +302,8 @@
 
         lax.fori_loop(0, (TR + 16) // rows, advance, 0)
 
-    pairs = [(j, k) for k in range(ITERS) for j in range(k + 1)]
-    sums = len(pairs) + ITERS
+    orders = 2 * ITERS - 1
+    sums = orders + ITERS
 
     def fold(value):
         total = value[:, 0:LANES]
@@ -293,7 +322,9 @@
         for k in range(2, ITERS):
             w.append(2.0 * y[k - 1] - w[k - 2])
         applied = [w[k] - y[k] for k in range(ITERS)]
-        fresh = [fold(v[j] * applied[k]) for j, k in pairs] + [fold(w[0] * v[k]) for k in range(ITERS)]
+        fresh = [fold(v[0] * applied[k]) for k in range(ITERS)]
+        fresh += [fold(v[ITERS - 1] * applied[k]) for k in range(1, ITERS)]
+        fresh += [fold(w[0] * v[k]) for k in range(ITERS)]
         return tuple(a + b for a, b in zip(carry, fresh))
 
     totals = lax.fori_loop(0, TR // 8, gram, tuple(jnp.zeros((8, LANES), F32) for _ in range(sums)))
@@ -318,10 +349,12 @@
     number = [total[n : n + 1, :] for n in range(sums)]
 
     matrix = [[None] * (ITERS + 1) for _ in range(ITERS)]
-    for n, (j, k) in enumerate(pairs):
-        matrix[j][k] = matrix[k][j] = number[n]
-    for k in range(ITERS):
-        matrix[k][ITERS] = number[len(pairs) + k]
+    for n in range(ITERS, orders):
+        number[n] = 2.0 * number[n] - number[2 * (ITERS - 1) - n]
+    for j in range(ITERS):
+        for k in range(j + 1):
+            matrix[j][k] = matrix[k][j] = 0.5 * (number[j + k] + number[j - k])
+        matrix[j][ITERS] = number[orders + j]
     for i in range(ITERS):
         inverse = 1.0 / matrix[i][i]
         for k in range(i + 1, ITERS + 1):
@@ -336,18 +369,20 @@
             coef[i] = coef[i] - matrix[i][k] * coef[k]
 
     def finish(i, carry):
-        at = pl.ds(pl.multiple_of(i * step, step), step)
-        inner = pl.ds(pl.multiple_of(16 + i * step, 8), step)
+        at = pl.ds(pl.multiple_of(i * half_step, half_step), half_step)
+        inner = pl.ds(pl.multiple_of(16 + i * half_step, 8), half_step)
         value = coef[0] * V[0, inner, 0:TC]
         for k in range(1, ITERS):
             value = value + coef[k] * V[k, inner, 0:TC]
-        x_out[at, :] = value
+        xv[at, :] = value
         high, low = halves(value)
-        seen = dot(high.astype(BF16), B[...]) + dot(low.astype(BF16), B[...])
-        place = lax.broadcasted_iota(jnp.int32, (step, S), 0) + i * step
+        both = dot(jnp.concatenate([high.astype(BF16), low.astype(BF16)], axis=0), B[...])
+        seen = both[:half_step] + both[half_step:]
+        place = lax.broadcasted_iota(jnp.int32, (half_step, S), 0) + i * half_step
         return carry + jnp.sum(jnp.where(place == fine_row, seen, 0.0), axis=0, keepdims=True)
 
-    at_fine = lax.fori_loop(0, TR // step, finish, jnp.zeros((1, S), F32))
+    at_fine = lax.fori_loop(0, TR // half_step, finish, jnp.zeros((1, S), F32))
+    store = pltpu.make_async_copy(xv, x_out, load_sem.at[8])
     for o in range(C):
         fval_out[o] = at_fine[:, o * per : (o + 1) * per]
     fval_in[col] = fval_out[col]
@@ -356,6 +391,7 @@
         for d in range(1, C)
     ]
 
+    store.start()
     place = lax.broadcasted_iota(jnp.int32, (BR, BC), 1)
     place_v = lax.broadcasted_iota(jnp.int32, (BR, BC), 0)
     within = remainder(place, GROUP)
@@ -365,15 +401,18 @@
         below = jnp.where(
             place_v == BR - 1, keep(bot_ok, crow_bot[n, 0:1, :]), pltpu.roll(volt, BR - 1, 0)
         )
-        far_left, far_right = cleft[n], cright[n]
-        turned_left = jnp.where(place == 0, 0.0, pltpu.roll(far_left, 1, 1))
-        plain_left = pltpu.roll(far_left, BC - GROUP + 1, 1)
-        from_left = jnp.where(left_ok, plain_left, turned_left)
-        turned_right = jnp.where(place == BC - 1, 0.0, pltpu.roll(far_right, BC - 1, 1))
-        plain_right = pltpu.roll(far_right, GROUP - 1, 1)
-        from_right = jnp.where(right_ok, plain_right, turned_right)
-        before = jnp.where(within == 0, from_left, pltpu.roll(volt, 1, 1))
-        after = jnp.where(within == GROUP - 1, from_right, pltpu.roll(volt, BC - 1, 1))
+        group = lax.broadcasted_iota(jnp.int32, (groups, BR), 0)
+        far = cleft[n]
+        turn[n, pl.ds(0, groups, stride=GROUP), :] = jnp.where(
+            left_ok, far, jnp.where(group == 0, 0.0, jnp.roll(far, 1, 0))
+        )
+        far = cright[n]
+        turn[n, pl.ds(GROUP - 1, groups, stride=GROUP), :] = jnp.where(
+            right_ok, far, jnp.where(group == groups - 1, 0.0, jnp.roll(far, -1, 0))
+        )
+        edge = turn[n].T
+        before = jnp.where(within == 0, edge, pltpu.roll(volt, 1, 1))
+        after = jnp.where(within == GROUP - 1, edge, pltpu.roll(volt, BC - 1, 1))
         return above + below + before + after
 
     for copy in coarse0:
@@ -388,11 +427,13 @@
     sources = onto_coarse(hi) + onto_coarse(lo)
     volt = partial + scale * sources
     volt1[...] = volt
+    seams(volt, 1)
     coarse1 = coarse_send(volt1, 1)
     partial = volt + scale * (sources - coarse_diag * volt)
     for copy in coarse1:
         copy.wait_recv()
     c_out[...] = partial + scale * (coarse_conductance * beside(volt, 1))
+    store.wait()
     for copy in pending:
         copy.wait_send()
 
@@ -408,9 +449,13 @@
     return pl.pallas_call(
         functools.partial(kernel, R, C),
         out_shape=(jax.ShapeDtypeStruct((TR, TC), F32), jax.ShapeDtypeStruct((BR, BC), F32)),
-        in_specs=[vmem] * 7 + [pl.BlockSpec(memory_space=pltpu.SMEM)],
-        out_specs=(vmem, vmem),
+        in_specs=[pl.BlockSpec(memory_space=pltpu.HBM)] * 8,
+        out_specs=(pl.BlockSpec(memory_space=pltpu.HBM), vmem),
         scratch_shapes=[
+            pltpu.VMEM((TR, TC), F32), pltpu.VMEM((TR, TC), jnp.int32), pltpu.VMEM((TR, TC), F32),
+            pltpu.VMEM((BR, BC), F32), pltpu.VMEM((BR, BC), F32),
+            pltpu.VMEM((1, S), jnp.int32), pltpu.VMEM((1, S), jnp.int32),
+            pltpu.SMEM((1, C), jnp.int32), pltpu.SemaphoreType.DMA((9,)), pltpu.VMEM((TR, TC), F32),
             pltpu.VMEM((C, 8, per), F32), pltpu.VMEM((C, 8, per), F32),
             pltpu.VMEM((C, 1, per), F32), pltpu.VMEM((C, 1, per), F32),
             pltpu.VMEM((C, 1, per), F32), pltpu.VMEM((C, 1, per), F32),
@@ -429,13 +474,14 @@
             pltpu.VMEM((16, LANES), F32), pltpu.VMEM((C - 1, 16, LANES), F32),
             pltpu.VMEM((16, LANES), F32), pltpu.VMEM((R - 1, 16, LANES), F32),
             pltpu.VMEM((BR, BC), F32),
+            pltpu.VMEM((2, BC, BR), F32), pltpu.VMEM((2, 2, BC // GROUP, BR), F32),
             pltpu.VMEM((2, 8, BC), F32), pltpu.VMEM((2, 8, BC), F32),
-            pltpu.VMEM((2, BR, BC), F32), pltpu.VMEM((2, BR, BC), F32),
+            pltpu.VMEM((2, BC // GROUP, BR), F32), pltpu.VMEM((2, BC // GROUP, BR), F32),
             pltpu.SemaphoreType.DMA((copies,)),
             pltpu.SemaphoreType.DMA((copies,)),
         ],
         compiler_params=pltpu.CompilerParams(
-            collective_id=0, has_side_effects=True, vmem_limit_bytes=48 * 1024 * 1024
+            collective_id=0, has_side_effects=True, vmem_limit_bytes=60 * 1024 * 1024
         ),
     )(load_amp, load_mask, leak, coarse_leak, coarse_init, via_fine, via_coarse, via_count)
 

time: 60.4 us -> 50.2 us (0.83)
  local copies, waits for them, and re-layouts: 8.97 us -> 2.93 us
  Pallas kernels: 50.4 us -> 46.5 us
    unnamed x18 -> x4, local copies, waits for them, and re-layouts: 8.97 us -> 2.93 us
    pallas_call x1, Pallas kernels: 50.4 us -> 46.5 us  [per_device(): pl.pallas_call(functools.partial(kernel, R, C), out_shape=(jax.ShapeDtype...]
where the time goes in v2:
time: 50.2 us; the launch traced here: 50 us
  Pallas kernels  46.5 us (93%)
  local copies, waits for them, and re-layouts  2.93 us (6%)
  between operations  0.65 us (1%)
    pallas_call x1, Pallas kernels, per_device(): pl.pallas_call(functools.partial(kernel, R, C), out_shape=(jax.ShapeDtype...  46.5 us
    unnamed x4, local copies, waits for them, and re-layouts  2.93 us

profile of v2, /device:TPU:0, one launch (start us, length us, event | category | flops | bytes accessed | tf_op | source)
XLA Modules:
  0.0 50.0 jit_solution(8327829001598012767)
XLA Ops:
  0.6 46.5 %shard_map.95 = (f32[512,512]{1,0:T(8,128)}, f32[128,128]{1,0:T(8,128)}) custom-call(f32[512,512]{1,0:T(8,128)} %amp_in.1, s32[512,512]{1,0:T(8,128)} %mask_in.1, f32[512,512]{1,0:T(8,128)} %leak_in.1, f32[128,128]{1,0:T(8,128)} %cleak_in.1, f32[128,128]{1,0:T(8,128)} %cinit_in.1, s32[1,1024]{1,0:T(1,128)} %vf_in.1, s32[1,1024]{1,0:T(1,128)} %vc_in.1, ...), custom_call_target="tpu_custom_call" | custom-call | tf_op jit(solution)/shard_map/pallas_call | solution.py:449
  47.1 0.0 copy-start
  47.1 2.3 %copy.12 = f32[512,512]{1,0:T(8,128)} copy(f32[512,512]{1,0:T(8,128)} %get-tuple-element.4) | data formatting | bytes 2097152
  49.4 0.0 copy-done
  49.4 0.6 %copy.13 = f32[128,128]{1,0:T(8,128)} copy(f32[128,128]{1,0:T(8,128)S(1)} %copy-done) | data formatting | bytes 131072
Async XLA Ops:
  47.1 2.3 %copy-start = (f32[128,128]{1,0:T(8,128)S(1)}, f32[128,128]{1,0:T(8,128)}, u32[]{:S(2)}) copy-start(f32[128,128]{1,0:T(8,128)} %get-tuple-element.5) | copy-start | bytes 196612

commit v3 on v2

--- a/solution.py
+++ b/solution.py
@@ -283,9 +283,9 @@
     width = TC + LANES
 
     def around(k, start, size):
-        tall = V.at[k, pl.ds(pl.multiple_of(start - 8, 8), size + 16), :]
-        mid = tall[8 : 8 + size, :]
-        total = tall[7 : 7 + size, :] + tall[9 : 9 + size, :]
+        tall = V[k, pl.ds(pl.multiple_of(start - 8, 8), size + 16), :]
+        mid = tall[8 : 8 + size]
+        total = pltpu.roll(tall, 1, 0)[8 : 8 + size] + pltpu.roll(tall, size + 15, 0)[8 : 8 + size]
         return total + pltpu.roll(mid, 1, 1) + pltpu.roll(mid, width - 1, 1)
 
     for k in range(ITERS - 1):
@@ -334,6 +334,19 @@
     copies = [
         send(red_out, red_in.at[d - 1], (row, lax.rem(col + d, C))) for d in range(1, C)
     ]
+
+    def gather(k):
+        def body(i, carry):
+            inner = pl.ds(pl.multiple_of(16 + i * half_step, 8), half_step)
+            high, low = halves(V[k, inner, 0:TC])
+            both = dot(jnp.concatenate([high.astype(BF16), low.astype(BF16)], axis=0), B[...])
+            seen = both[:half_step] + both[half_step:]
+            place = lax.broadcasted_iota(jnp.int32, (half_step, S), 0) + i * half_step
+            return carry + jnp.sum(jnp.where(place == fine_row, seen, 0.0), axis=0, keepdims=True)
+
+        return lax.fori_loop(0, TR // half_step, body, jnp.zeros((1, S), F32))
+
+    seen_at = [gather(k) for k in range(ITERS // 2)]
     total = red_out[...]
     for d, copy in enumerate(copies):
         copy.wait_recv()
@@ -342,6 +355,7 @@
     copies = [
         send(red2_out, red2_in.at[d - 1], (lax.rem(row + d, R), col)) for d in range(1, R)
     ]
+    seen_at += [gather(k) for k in range(ITERS // 2, ITERS)]
     for d, copy in enumerate(copies):
         copy.wait_recv()
         total = total + red2_in[d]
@@ -368,20 +382,9 @@
         for k in range(i + 1, ITERS):
             coef[i] = coef[i] - matrix[i][k] * coef[k]
 
-    def finish(i, carry):
-        at = pl.ds(pl.multiple_of(i * half_step, half_step), half_step)
-        inner = pl.ds(pl.multiple_of(16 + i * half_step, 8), half_step)
-        value = coef[0] * V[0, inner, 0:TC]
-        for k in range(1, ITERS):
-            value = value + coef[k] * V[k, inner, 0:TC]
-        xv[at, :] = value
-        high, low = halves(value)
-        both = dot(jnp.concatenate([high.astype(BF16), low.astype(BF16)], axis=0), B[...])
-        seen = both[:half_step] + both[half_step:]
-        place = lax.broadcasted_iota(jnp.int32, (half_step, S), 0) + i * half_step
-        return carry + jnp.sum(jnp.where(place == fine_row, seen, 0.0), axis=0, keepdims=True)
-
-    at_fine = lax.fori_loop(0, TR // half_step, finish, jnp.zeros((1, S), F32))
+    at_fine = coef[0] * seen_at[0]
+    for k in range(1, ITERS):
+        at_fine = at_fine + coef[k] * seen_at[k]
     store = pltpu.make_async_copy(xv, x_out, load_sem.at[8])
     for o in range(C):
         fval_out[o] = at_fine[:, o * per : (o + 1) * per]
@@ -391,6 +394,17 @@
         for d in range(1, C)
     ]
 
+
+    def finish(i, carry):
+        at = pl.ds(pl.multiple_of(i * step, step), step)
+        inner = pl.ds(pl.multiple_of(16 + i * step, 8), step)
+        value = coef[0] * V[0, inner, 0:TC]
+        for k in range(1, ITERS):
+            value = value + coef[k] * V[k, inner, 0:TC]
+        xv[at, :] = value
+        return carry
+
+    lax.fori_loop(0, TR // step, finish, 0)
     store.start()
     place = lax.broadcasted_iota(jnp.int32, (BR, BC), 1)
     place_v = lax.broadcasted_iota(jnp.int32, (BR, BC), 0)

time: 50.2 us -> 49.1 us (0.978)
  Pallas kernels: 46.5 us -> 45.3 us
    pallas_call x1, Pallas kernels: 46.5 us -> 45.3 us  [per_device(): pl.pallas_call(functools.partial(kernel, R, C), out_shape=(jax.ShapeDtype...]
where the time goes in v3:
time: 49.1 us; the launch traced here: 48.9 us
  Pallas kernels  45.3 us (92%)
  local copies, waits for them, and re-layouts  2.93 us (6%)
  between operations  0.65 us (1%)
    pallas_call x1, Pallas kernels, per_device(): pl.pallas_call(functools.partial(kernel, R, C), out_shape=(jax.ShapeDtype...  45.3 us
    unnamed x4, local copies, waits for them, and re-layouts  2.93 us

profile of v3, /device:TPU:0, one launch (start us, length us, event | category | flops | bytes accessed | tf_op | source)
XLA Modules:
  0.0 48.9 jit_solution(14116704387941271139)
XLA Ops:
  0.6 45.3 %shard_map.95 = (f32[512,512]{1,0:T(8,128)}, f32[128,128]{1,0:T(8,128)}) custom-call(f32[512,512]{1,0:T(8,128)} %amp_in.1, s32[512,512]{1,0:T(8,128)} %mask_in.1, f32[512,512]{1,0:T(8,128)} %leak_in.1, f32[128,128]{1,0:T(8,128)} %cleak_in.1, f32[128,128]{1,0:T(8,128)} %cinit_in.1, s32[1,1024]{1,0:T(1,128)} %vf_in.1, s32[1,1024]{1,0:T(1,128)} %vc_in.1, ...), custom_call_target="tpu_custom_call" | custom-call | tf_op jit(solution)/shard_map/pallas_call | solution.py:463
  46.0 0.0 copy-start
  46.0 2.3 %copy.12 = f32[512,512]{1,0:T(8,128)} copy(f32[512,512]{1,0:T(8,128)} %get-tuple-element.4) | data formatting | bytes 2097152
  48.3 0.0 copy-done
  48.3 0.6 %copy.13 = f32[128,128]{1,0:T(8,128)} copy(f32[128,128]{1,0:T(8,128)S(1)} %copy-done) | data formatting | bytes 131072
Async XLA Ops:
  46.0 2.3 %copy-start = (f32[128,128]{1,0:T(8,128)S(1)}, f32[128,128]{1,0:T(8,128)}, u32[]{:S(2)}) copy-start(f32[128,128]{1,0:T(8,128)} %get-tuple-element.5) | copy-start | bytes 196612
